TPU v7x, 256 devices: a whole 4x4x8 slice. The times are simulated.
256 devices in a mesh: seq: 128 (over x, y, z), resp: 2 (over core).
Axes of the slice: x: 4, y: 4, z: 8, core: 2. Of those that a mesh axis runs over, the one named last changes fastest.
Arguments:
- cat_query: bfloat16 [16384, 4096], P('seq', 'resp'), may hold values from -6 to 6
- cat_key: bfloat16 [16384, 4096], P('seq', 'resp'), may hold values from -6 to 6
- cat_value: bfloat16 [16384, 4096], P('seq', 'resp'), may hold values from -6 to 6
- resp_query: bfloat16 [32768, 4096], P(('seq', 'resp')), may hold values from -6 to 6
- resp_key: bfloat16 [32768, 4096], P(('seq', 'resp')), may hold values from -6 to 6
- resp_value: bfloat16 [32768, 4096], P(('seq', 'resp')), may hold values from -6 to 6
- resp_lengths: int32 [256, 3], P(('seq', 'resp')), may hold values from 1 to 64, 128 in all within a row
- norm_gain: float32 [4096], replicated, may hold values from 0.1 to 1.9
Outputs:
- cat_out: bfloat16 [16384, 4096], P('seq', 'resp')
- resp_out: bfloat16 [32768, 4096], P(('seq', 'resp'))
Inputs may be any that keep to these rules, and one draw needn't show every extreme that they name: `resp_lengths`: each row's 3 lengths sum to 128.
All inputs are finite; a program needn't handle non-finite values.
Results may differ from a plain program's by a relative error of at most 0.0021.
Values sent between devices are 32-bit elements; how exact they have to be, the bound alone decides.
A program may use at most 320 MiB of HBM per device.

v0:
```python
import jax
import jax.numpy as jnp
from jax import lax
from jax.sharding import PartitionSpec as P

DH = 128


def attend_inner(query, key, value, mask, heads):
    rows = query.shape[0]
    qh = query.reshape(rows, heads, DH)
    kh = key.reshape(rows, heads, DH)
    vh = value.reshape(rows, heads, DH)
    scores = jnp.einsum("thd,shd->hts", qh, kh, preferred_element_type=jnp.float32)
    scores = jnp.where(mask[None, :, :], scores, 0.0).astype(jnp.bfloat16)
    return jnp.einsum("hts,shd->thd", scores, vh, preferred_element_type=jnp.float32)


def attend_outer(query, state, heads):
    rows = query.shape[0]
    qh = query.reshape(rows, heads, DH).astype(jnp.float32)
    return jnp.einsum("thd,hde->the", qh, state, precision=lax.Precision.HIGHEST)


def block_state(key, value, heads):
    rows = key.shape[0]
    kh = key.reshape(rows, heads, DH)
    vh = value.reshape(rows, heads, DH)
    return jnp.einsum("shd,she->hde", kh, vh, preferred_element_type=jnp.float32)


def head_norm(raw, gain, heads):
    square = jnp.mean(raw * raw, axis=-1, keepdims=True)
    scaled = raw * lax.rsqrt(square + 1e-06) * gain.reshape(heads, DH)
    return scaled.reshape(raw.shape[0], heads * DH).astype(jnp.bfloat16)


def transpose_scan(local_state):
    peers = lax.axis_size("seq")
    chunks = local_state.reshape(peers, -1, DH)
    gathered = lax.all_to_all(chunks, "seq", 0, 0, tiled=True)
    before = lax.broadcasted_iota(jnp.int32, (peers, peers), 1) < lax.broadcasted_iota(
        jnp.int32, (peers, peers), 0
    )
    flat = gathered.reshape(peers, -1)
    exclusive = jnp.dot(before.astype(jnp.float32), flat, precision=lax.Precision.HIGHEST).reshape(
        chunks.shape
    )
    prefix = lax.all_to_all(exclusive, "seq", 0, 0, tiled=True)
    return prefix.reshape(local_state.shape)


def per_device(
    cat_query, cat_key, cat_value, resp_query, resp_key, resp_value, resp_lengths, norm_gain
):
    heads_here = cat_query.shape[1] // DH
    all_heads = resp_query.shape[1] // DH
    local_state = block_state(cat_key, cat_value, heads_here)
    total = lax.psum(local_state, "seq")
    prefix = transpose_scan(local_state)
    whole = lax.all_gather(total, "resp", axis=0, tiled=True)
    places = jnp.arange(cat_query.shape[0], dtype=jnp.int32)
    causal = places[None, :] <= places[:, None]
    cat_inner = attend_inner(cat_query, cat_key, cat_value, causal, heads_here)
    rows = jnp.arange(resp_query.shape[0], dtype=jnp.int32)
    ends = jnp.cumsum(resp_lengths[0])
    segment = jnp.sum((rows[:, None] >= ends[None, :]).astype(jnp.int32), axis=1)
    mask = (segment[:, None] == segment[None, :]) & (rows[None, :] <= rows[:, None])
    resp_inner = attend_inner(resp_query, resp_key, resp_value, mask, all_heads)
    cat_raw = cat_inner + attend_outer(cat_query, prefix, heads_here)
    offset = lax.axis_index("resp") * (heads_here * DH)
    cat_gain = lax.dynamic_slice_in_dim(norm_gain, offset, heads_here * DH)
    cat_out = head_norm(cat_raw, cat_gain, heads_here)
    resp_raw = resp_inner + attend_outer(resp_query, whole, all_heads)
    resp_out = head_norm(resp_raw, norm_gain, all_heads)
    return (cat_out, resp_out)


def solution(mesh):
    placed = (
        P("seq", "resp"),
        P("seq", "resp"),
        P("seq", "resp"),
        P(("seq", "resp"), None),
        P(("seq", "resp"), None),
        P(("seq", "resp"), None),
        P(("seq", "resp"), None),
        P(),
    )
    return jax.shard_map(
        per_device,
        mesh=mesh,
        in_specs=placed,
        out_specs=(P("seq", "resp"), P(("seq", "resp"), None)),
        check_vma=False,
    )
```

profile of v0, /device:TPU:32, one launch (start us, length us, event | category | flops | bytes accessed | tf_op | source)
XLA Modules:
  0.0 308.4 jit_solution(7206592568741554956)
XLA Ops:
  7.2 0.0 copy-start
  7.2 1.4 copy.68
  8.6 0.0 copy-start.1
  8.6 2.5 fusion.18
  11.1 15.0 %all-to-all-start = ((f32[128,16,128]{2,1,0:T(8,128)}), f32[128,16,128]{2,1,0:T(8,128)S(1)}, u32[]{:S(2)}, u32[]{:S(2)}) async-start(f32[128,16,128]{2,1,0:T(8,128)} %bitcast.2), calls=%async_computation | async-start | bytes 2097152 | tf_op jit(solution)/shard_map/all_to_all | solution.py:41
  26.1 0.0 all-reduce.2.cloned.1.call-start
  26.2 0.7 all-reduce.2.cloned.1.call-update
  26.8 0.0 all-gather.2.cloned.1.call-start
  26.9 227.3 %all-reduce.2.cloned.1.call-done = f32[16,128,128]{2,1,0:T(8,128)} async-done(((f32[16,128,128]{2,1,0:T(8,128)}), f32[16,128,128]{2,1,0:T(8,128)}) %all-reduce.2.cloned.1.call-update) | async-done | bytes 1048592 | tf_op jit(solution)/shard_map/psum | solution.py:59
  254.1 0.0 all-gather.2.cloned.1.call-update
  254.2 0.4 copy.66
  254.6 0.7 fusion.10
  255.3 0.0 copy-start.6
  255.3 0.0 copy-start.4
  255.3 1.6 copy.54
  256.9 11.3 %all-to-all-start.1 = ((f32[128,16,128]{2,1,0:T(8,128)}), f32[128,16,128]{2,1,0:T(8,128)}, u32[]{:S(2)}, u32[]{:S(2)}) async-start(f32[128,16,128]{2,1,0:T(8,128)} %copy.54), calls=%async_computation.1 | async-start | bytes 2097152 | tf_op jit(solution)/shard_map/all_to_all | solution.py:49
  268.3 0.2 reduce-window.8
  268.4 1.3 copy.67
  269.8 0.1 convert_reduce_fusion
  269.9 0.1 compare_and_fusion
  270.0 3.1 %fusion = f32[32,128,128]{1,2,0:T(8,128)S(1)} fusion(bf16[128,32,128]{0,2,1:T(8,128)(2,1)} %bitcast.93, pred[128,128]{1,0:T(8,128)(4,1)S(1)} %compare_and_fusion, bf16[128,4096]{1,0:T(8,128)(2,1)} %param.12, bf16[128,4096]{1,0:T(8,128)(2,1)S(1)} %copy-done), kind=kOutput, calls=%fused_computation.5 | convolution fusion | flops 269484032 | bytes 5259264 | tf_op jit(solution)/shard_map/hts,shd->thd/dot_general | solution.py:16
  273.1 0.0 all-gather.2.cloned.1.call-done
  273.1 3.5 %multiply_reduce_fusion = (f32[128,32]{0,1:T(8,128)S(1)}, f32[128,32,128]{0,2,1:T(8,128)S(1)}) fusion(f32[32,128,128]{2,1,0:T(8,128)} %all-gather.2.cloned.1.call-done, f32[32,128,128]{1,2,0:T(8,128)S(1)} %fusion, bf16[128,4096]{1,0:T(8,128)(2,1)S(1)} %copy-done), kind=kOutput, calls=%fused_computation.2 | convolution fusion | flops 806875136 | bytes 7356416 | tf_op jit(solution)/shard_map/thd,hde->the/dot_general | solution.py:22
  276.6 0.0 copy-start.3
  276.6 0.7 multiply_convert_fusion
  277.3 0.0 copy-start.2
  277.4 1.3 copy.63
  278.7 16.2 %all-to-all-done.1 = f32[128,16,128]{2,1,0:T(8,128)} async-done(((f32[128,16,128]{2,1,0:T(8,128)}), f32[128,16,128]{2,1,0:T(8,128)}, u32[]{:S(2)}, u32[]{:S(2)}) %all-to-all-start.1) | async-done | bytes 1048608 | tf_op jit(solution)/shard_map/all_to_all | solution.py:49
  294.9 3.2 %convolution_bitcast_fusion.1 = f32[128,16,128]{0,2,1:T(8,128)} fusion(f32[16,128,128]{2,1,0:T(8,128)} %bitcast.6, bf16[128,2048]{1,0:T(8,128)(2,1)S(1)} %copy-done.3), kind=kOutput, calls=%fused_computation.8 | convolution fusion | flops 402653184 | bytes 2621440 | tf_op jit(solution)/shard_map/thd,hde->the/dot_general | solution.py:22
  298.1 2.1 multiply_reduce_fusion.1
  300.2 0.3 multiply_convert_fusion.1
  300.5 1.0 copy.62
  (13 shorter events, 0.1 us)
Async XLA Ops:
  7.2 262.8 %copy-start = (bf16[128,4096]{1,0:T(8,128)(2,1)S(1)}, bf16[128,4096]{1,0:T(8,128)(2,1)}, u32[]{:S(2)}) copy-start(bf16[128,4096]{1,0:T(8,128)(2,1)} %param.11) | copy-start | bytes 3145732
  8.6 2.5 copy-start.1
  11.1 243.1 %all-to-all-start = ((f32[128,16,128]{2,1,0:T(8,128)}), f32[128,16,128]{2,1,0:T(8,128)S(1)}, u32[]{:S(2)}, u32[]{:S(2)}) async-start(f32[128,16,128]{2,1,0:T(8,128)} %bitcast.2), calls=%async_computation | async-start | bytes 2097152 | tf_op jit(solution)/shard_map/all_to_all | solution.py:41
  26.1 228.0 %all-reduce.2.cloned.1.call-start = ((), (), s32[]{:S(2)}) async-start(), calls=%async_computation.2 | async-start | bytes 2097152 | tf_op jit(solution)/shard_map/psum | solution.py:59
  26.8 246.2 %all-gather.2.cloned.1.call-start = ((), (), s32[]{:S(2)}) async-start(), calls=%async_computation.3 | async-start | bytes 3145728 | tf_op jit(solution)/shard_map/all_gather | solution.py:61
  255.3 13.0 %copy-start.6 = (s32[1,3]{1,0:T(1,128)S(1)}, s32[1,3]{1,0:T(1,128)}, u32[]{:S(2)}) copy-start(s32[1,3]{1,0:T(1,128)} %param.14) | copy-start | bytes 40
  255.3 13.1 %copy-start.4 = (bf16[128,4096]{1,0:T(8,128)(2,1)S(1)}, bf16[128,4096]{1,0:T(8,128)(2,1)}, u32[]{:S(2)}) copy-start(bf16[128,4096]{1,0:T(8,128)(2,1)} %param.13) | copy-start | bytes 3145732
  256.9 12.8 %copy-start.5 = (f32[4096]{0:T(1024)S(1)}, f32[4096]{0:T(1024)}, u32[]{:S(2)}) copy-start(f32[4096]{0:T(1024)} %param.15) | copy-start | bytes 49156
  256.9 38.0 %all-to-all-start.1 = ((f32[128,16,128]{2,1,0:T(8,128)}), f32[128,16,128]{2,1,0:T(8,128)}, u32[]{:S(2)}, u32[]{:S(2)}) async-start(f32[128,16,128]{2,1,0:T(8,128)} %copy.54), calls=%async_computation.1 | async-start | bytes 2097152 | tf_op jit(solution)/shard_map/all_to_all | solution.py:49
  276.6 18.3 %copy-start.3 = (bf16[128,2048]{1,0:T(8,128)(2,1)S(1)}, bf16[128,2048]{1,0:T(8,128)(2,1)}, u32[]{:S(2)}) copy-start(bf16[128,2048]{1,0:T(8,128)(2,1)} %param.8) | copy-start | bytes 1572868
  277.3 20.8 %copy-start.2 = (bf16[128,2048]{0,1:T(8,128)(2,1)S(1)}, bf16[128,2048]{0,1:T(8,128)(2,1)}, u32[]{:S(2)}) copy-start(bf16[128,2048]{0,1:T(8,128)(2,1)} %copy-done.1) | copy-start | bytes 1572868
Sparse Core Ops, SparseCore 0:
  32.9 221.2 all-reduce.1
  255.9 14.2 all-gather.1
where the time goes:
time: 309 us; the launch traced here: 308 us
  waiting for transfers between devices  244 us (79%)
  starting transfers between devices  26.4 us (9%)
  matrix products  15 us (5%)
  between operations  14.2 us (5%)
  local copies, waits for them, and re-layouts  7.08 us (2%)
    psum x1, waiting for transfers between devices, per_device(): total = lax.psum(local_state, 'seq')  227 us
    all_to_all x1, waiting for transfers between devices, transpose_scan(): prefix = lax.all_to_all(exclusive, 'seq', 0, 0, tiled=True)  16.2 us
    all_to_all x1, starting transfers between devices, transpose_scan(): gathered = lax.all_to_all(chunks, 'seq', 0, 0, tiled=True)  15 us
    all_to_all x1, starting transfers between devices, transpose_scan(): prefix = lax.all_to_all(exclusive, 'seq', 0, 0, tiled=True)  11.3 us
    dot_general x2, matrix products, attend_outer(): jnp.einsum('thd,hde->the', qh, state, precision=lax.Precision.HIGHEST)  6.68 us
  transfers between devices with their start and end apart: 4, of which 2 were waited for; matrix products, arithmetic and copies ran while one was open for 4% of the time, Pallas kernels for 0%

commit v1 on v0

--- a/solution.py
+++ b/solution.py
@@ -56,7 +56,7 @@
     heads_here = cat_query.shape[1] // DH
     all_heads = resp_query.shape[1] // DH
     local_state = block_state(cat_key, cat_value, heads_here)
-    total = lax.psum(local_state, "seq")
+    total = jnp.sum(lax.all_gather(local_state, "seq"), axis=0)
     prefix = transpose_scan(local_state)
     whole = lax.all_gather(total, "resp", axis=0, tiled=True)
     places = jnp.arange(cat_query.shape[0], dtype=jnp.int32)

time: 309 us -> 716 us (2.32)
  waiting for transfers between devices: 244 us -> 564 us
  blocking collectives: 0 us -> 56.1 us
  other arithmetic: 1.44 us -> 45.1 us
  starting transfers between devices: 26.4 us -> 8.15 us
    all_gather x0 -> x1, waiting for transfers between devices: none -> 564 us  [per_device(): total = jnp.sum(lax.all_gather(local_state, 'seq'), axis=0)]
    psum x1 -> x0, waiting for transfers between devices: 227 us -> none  [per_device(): total = lax.psum(local_state, 'seq')]
    all_to_all x0 -> x1, blocking collectives: none -> 56.1 us  [transpose_scan(): gathered = lax.all_to_all(chunks, 'seq', 0, 0, tiled=True)]
    reduce_sum x0 -> x1, other arithmetic: none -> 41.6 us  [per_device(): total = jnp.sum(lax.all_gather(local_state, 'seq'), axis=0)]
    all_to_all x1, waiting for transfers between devices: 16.2 us -> 0.01 us  [transpose_scan(): prefix = lax.all_to_all(exclusive, 'seq', 0, 0, tiled=True)]
    all_to_all x1 -> x0, starting transfers between devices: 15 us -> none  [transpose_scan(): gathered = lax.all_to_all(chunks, 'seq', 0, 0, tiled=True)]
  transfers between devices with their start and end apart: 4 -> 3, of which waited for: 2 -> 1; matrix products, arithmetic and copies ran while one was open for 4% -> 9% of each run, Pallas kernels for 0% -> 0%
where the time goes in v1:
time: 716 us; the launch traced here: 713 us
  waiting for transfers between devices  564 us (79%)
  blocking collectives  56.1 us (8%)
  other arithmetic  45.1 us (6%)
  matrix products  16.4 us (2%)
  between operations  14.1 us (2%)
  local copies, waits for them, and re-layouts  9.26 us (1%)
  starting transfers between devices  8.15 us (1%)
    all_gather x1, waiting for transfers between devices, per_device(): total = jnp.sum(lax.all_gather(local_state, 'seq'), axis=0)  564 us
    all_to_all x1, blocking collectives, transpose_scan(): gathered = lax.all_to_all(chunks, 'seq', 0, 0, tiled=True)  56.1 us
    reduce_sum x1, other arithmetic, per_device(): total = jnp.sum(lax.all_gather(local_state, 'seq'), axis=0)  41.6 us
  transfers between devices with their start and end apart: 3, of which 1 were waited for; matrix products, arithmetic and copies ran while one was open for 9% of the time, Pallas kernels for 0%

profile of v1, /device:TPU:32, one launch (start us, length us, event | category | flops | bytes accessed | tf_op | source)
XLA Modules:
  0.0 713.0 jit_solution(10701000000541594741)
XLA Ops:
  7.2 0.0 copy-start
  7.2 0.0 all-gather.6.cloned.1.call-start
  7.2 1.4 copy.66
  8.6 0.0 copy-start.1
  8.6 2.5 fusion.18
  11.1 0.0 all-gather.6.cloned.1.call-update
  11.2 56.1 %all_to_all.10 = f32[128,16,128]{2,1,0:T(8,128)} all-to-all(f32[128,16,128]{2,1,0:T(8,128)} %bitcast.92), channel_id=1, replica_groups=mesh['seq'=128,'resp'=2] {'seq'}, dimensions={0} | all-to-all | bytes 2097152 | tf_op jit(solution)/shard_map/all_to_all | solution.py:41
  67.2 0.0 copy-done.1
  67.2 1.6 copy.64
  68.8 0.7 fusion.10
  69.5 1.6 copy.52
  71.1 7.9 %all-to-all-start.1 = ((f32[128,16,128]{2,1,0:T(8,128)}), f32[128,16,128]{2,1,0:T(8,128)}, u32[]{:S(2)}, u32[]{:S(2)}) async-start(f32[128,16,128]{2,1,0:T(8,128)} %copy.52), calls=%async_computation.1 | async-start | bytes 2097152 | tf_op jit(solution)/shard_map/all_to_all | solution.py:49
  79.0 0.2 all-gather.4.cloned.1.call-start
  79.2 563.8 %all-gather.6.cloned.1.call-done = f32[2048,128,128]{2,1,0:T(8,128)} async-done(((f32[16,128,128]{2,1,0:T(8,128)}), f32[2048,128,128]{2,1,0:T(8,128)}) %all-gather.6.cloned.1.call-update) | async-done | bytes 134217744 | tf_op jit(solution)/shard_map/all_gather | solution.py:59
  643.0 41.6 %reduce_sum.38 = f32[16,128,128]{2,1,0:T(8,128)} reduce(f32[128,16,128,128]{3,2,1,0:T(8,128)} %bitcast.14, f32[]{:T(128)} %constant.7.clone.1), dimensions={0}, to_apply=%region_3.4 | reduce | flops 33292288 | bytes 135266304 | tf_op jit(solution)/shard_map/reduce_sum | solution.py:59
  684.5 0.0 all-gather.4.cloned.1.call-update
  684.6 0.0 copy-done.2
  684.6 1.3 copy.65
  685.9 0.0 copy-done.4
  685.9 0.2 reduce-window.8
  686.1 0.0 copy-done.3
  686.1 0.1 convert_reduce_fusion
  686.2 0.1 compare_and_fusion
  686.3 3.1 fusion
  689.4 0.0 all-to-all-done.1
  689.4 3.3 convolution_bitcast_fusion.1
  692.7 3.3 multiply_reduce_fusion.1
  696.1 2.5 multiply_convert_fusion.1
  698.5 2.0 copy.60
  700.6 3.5 multiply_reduce_fusion
  704.1 0.7 multiply_convert_fusion
  704.8 1.3 copy.61
  (9 shorter events, 0.0 us)
Async XLA Ops:
  7.2 679.1 %copy-start = (bf16[128,4096]{1,0:T(8,128)(2,1)S(1)}, bf16[128,4096]{1,0:T(8,128)(2,1)}, u32[]{:S(2)}) copy-start(bf16[128,4096]{1,0:T(8,128)(2,1)} %param.11) | copy-start | bytes 3145732
  7.2 635.8 %all-gather.6.cloned.1.call-start = ((), (), s32[]{:S(2)}) async-start(), calls=%async_computation.3 | async-start | bytes 135266304 | tf_op jit(solution)/shard_map/all_gather | solution.py:59
  8.6 58.6 %copy-start.1 = (bf16[128,2048]{0,1:T(8,128)(2,1)}, bf16[128,2048]{0,1:T(8,128)(2,1)S(1)}, u32[]{:S(2)}) copy-start(bf16[128,2048]{0,1:T(8,128)(2,1)S(1)} %copy.66) | copy-start | bytes 1572868
  71.1 618.3 %all-to-all-start.1 = ((f32[128,16,128]{2,1,0:T(8,128)}), f32[128,16,128]{2,1,0:T(8,128)}, u32[]{:S(2)}, u32[]{:S(2)}) async-start(f32[128,16,128]{2,1,0:T(8,128)} %copy.52), calls=%async_computation.1 | async-start | bytes 2097152 | tf_op jit(solution)/shard_map/all_to_all | solution.py:49
  79.0 621.6 %all-gather.4.cloned.1.call-start = ((), (), s32[]{:S(2)}) async-start(), calls=%async_computation.2 | async-start | bytes 3145728 | tf_op jit(solution)/shard_map/all_gather | solution.py:61
  643.0 41.6 %copy-start.2 = (bf16[128,4096]{1,0:T(8,128)(2,1)S(1)}, bf16[128,4096]{1,0:T(8,128)(2,1)}, u32[]{:S(2)}) copy-start(bf16[128,4096]{1,0:T(8,128)(2,1)} %param.13) | copy-start | bytes 3145732
  684.5 1.4 copy-start.4
  684.5 1.5 copy-start.3
Sparse Core Ops, SparseCore 0:
  12.2 630.7 all-gather.5
  684.7 14.7 all-gather.3
